TPU v7x, 32 devices: a whole 2x2x4 slice. The times are simulated.
32 devices in a mesh: lat: 4 (over y, x), ord: 8 (over z, core).
Axes of the slice: x: 2, y: 2, z: 4, core: 2. Of those that a mesh axis runs over, the one named last changes fastest.
Arguments:
- heights: bfloat16 [512, 43200], P(('lat', 'ord')), may hold values from -1.5 to 1.5
- panels: bfloat16 [512, 5120, 128], P('lat', 'ord'), may hold values from -0.25 to 0.25
- ord_slot: int32 [5120], replicated, may hold values from 0 to 5119, each once
- cutoffs: int32 [5120], P('ord'), may hold values from 13360 to 21599
Outputs:
- gravity: float32 [512, 43200], P(('lat', 'ord'))
Inputs may be any that keep to these rules, and one draw needn't show every extreme that they name: `ord_slot`: a permutation of the order slots.
All inputs are finite; a program needn't handle non-finite values.
Results may differ from a plain program's by a relative error of at most 0.0039.
Values may be sent and summed in bfloat16 or wider, within the bound.
No kernel may reach another device: no remote copies, remote signals or barrier semaphores. Data moves between devices by JAX's collectives and lax.ppermute only.
A program may use at most 192 MiB of HBM per device.

v0:
```python
import math
import jax
import jax.numpy as jnp
from jax import lax
from jax.sharding import PartitionSpec as P

LON_SLOW = 180
LON_FAST = 240
ORDERS = 5120
DEG = 128
NMAX = 21600


def slow_tables(slow):
    index = jnp.arange(slow, dtype=jnp.int32)
    phase = index[:, None] * index[None, :] % slow
    angle = 2.0 * math.pi / slow * phase.astype(jnp.float32)
    return (jnp.cos(angle), jnp.sin(angle))


def twiddle_tables(slow, fast, blocks):
    total = slow * fast
    first = jnp.arange(slow, dtype=jnp.int32)[:, None, None]
    middle = jnp.arange(fast, dtype=jnp.int32)[None, :, None]
    last = jnp.arange(blocks, dtype=jnp.int32)[None, None, :]
    phase = (middle * first + slow * middle * last) % total
    angle = 2.0 * math.pi / total * phase.astype(jnp.float32)
    return (jnp.cos(angle), jnp.sin(angle))


def forward_spectra(values, slow, fast, orders):
    count = values.shape[0]
    grid = values.reshape(count, slow, fast)
    cosine, sine = slow_tables(slow)
    first_real = jnp.einsum("raj,ak->rkj", grid, cosine, precision=lax.Precision.HIGHEST)
    first_imag = -jnp.einsum("raj,ak->rkj", grid, sine, precision=lax.Precision.HIGHEST)
    blocks = orders // slow + 1
    twist_cos, twist_sin = twiddle_tables(slow, fast, blocks)
    joined = jnp.concatenate([first_real, first_imag], 2)
    table = jnp.concatenate(
        [jnp.concatenate([twist_cos, -twist_sin], 2), jnp.concatenate([twist_sin, twist_cos], 2)], 1
    )
    second = jnp.einsum("rkj,kjq->rkq", joined, table, precision=lax.Precision.HIGHEST)
    scale_in = 1.0 / math.sqrt(slow * fast)
    spec_real = (
        second[:, :, :blocks].transpose(0, 2, 1).reshape(count, blocks * slow)[:, 1 : orders + 1]
    )
    spec_imag = (
        second[:, :, blocks:].transpose(0, 2, 1).reshape(count, blocks * slow)[:, 1 : orders + 1]
    )
    return (spec_real * scale_in, spec_imag * scale_in)


def inverse_field(full_real, full_imag, slow, fast):
    count = full_real.shape[0]
    blocks = full_real.shape[1] // slow
    grid_real = full_real.reshape(count, blocks, slow).transpose(0, 2, 1)
    grid_imag = full_imag.reshape(count, blocks, slow).transpose(0, 2, 1)
    joined = jnp.concatenate([grid_real, grid_imag], 2)
    twist_cos, twist_sin = twiddle_tables(slow, fast, blocks)
    cos_turned = twist_cos.transpose(0, 2, 1)
    sin_turned = twist_sin.transpose(0, 2, 1)
    table = jnp.concatenate(
        [
            jnp.concatenate([cos_turned, sin_turned], 2),
            jnp.concatenate([-sin_turned, cos_turned], 2),
        ],
        1,
    )
    second = jnp.einsum("rkq,kqj->rkj", joined, table, precision=lax.Precision.HIGHEST)
    cosine, sine = slow_tables(slow)
    field = jnp.einsum("rkj,ka->raj", second[:, :, :fast], cosine, precision=lax.Precision.HIGHEST)
    field = field - jnp.einsum(
        "rkj,ka->raj", second[:, :, fast:], sine, precision=lax.Precision.HIGHEST
    )
    return field.reshape(count, slow * fast)


def fold_powers(terms, factors):
    slots = terms.shape[1]
    width = terms.shape[2]
    return jnp.sum(terms.reshape(3, 2, slots, width) * factors[:, None, None, :], axis=0)


def local(heights, panels, ord_slot, cutoffs):
    lat_count = lax.axis_size("lat")
    ord_count = lax.axis_size("ord")
    level = heights.astype(jnp.float32)
    cycle_dev = level.shape[0]
    square = level * level
    powers = jnp.concatenate([level, square, square * level], 0)
    spec_real, spec_imag = forward_spectra(powers, LON_SLOW, LON_FAST, ORDERS)
    picked = jnp.stack(
        [
            spec_real[:, ord_slot].reshape(3, cycle_dev, ORDERS),
            spec_imag[:, ord_slot].reshape(3, cycle_dev, ORDERS),
        ],
        1,
    )
    picked = picked.reshape(6, cycle_dev, ORDERS).astype(jnp.bfloat16)
    sums = jnp.einsum(
        "xrk,rkn->xkn",
        lax.all_to_all(picked, "ord", split_axis=2, concat_axis=1, tiled=True),
        panels,
        preferred_element_type=jnp.float32,
    )
    stride = (NMAX - ORDERS) // DEG
    degree_int = ORDERS + jnp.arange(DEG, dtype=jnp.int32) * stride
    degree = degree_int.astype(jnp.float32)
    factors = jnp.stack(
        [
            jnp.ones_like(degree),
            (degree + 2.0) / (2.0 * NMAX),
            (degree + 2.0) * (degree + 1.0) / (6.0 * NMAX * NMAX),
        ]
    )
    keep = (degree_int[None, :] <= cutoffs[:, None]).astype(jnp.float32)
    terms = fold_powers(sums, factors)
    total = lax.psum(terms, "lat")
    coeffs = (total * keep[None]).astype(jnp.bfloat16)
    synthesis = jnp.einsum("rkn,ckn->crk", panels, coeffs, preferred_element_type=jnp.float32)
    returned = lax.all_to_all(synthesis, "ord", split_axis=1, concat_axis=2, tiled=True)
    blocks = ORDERS // LON_SLOW + 1
    target = ord_slot + 1
    full_real = (
        jnp.zeros((cycle_dev, blocks * LON_SLOW), jnp.float32).at[:, target].set(returned[0])
    )
    full_imag = (
        jnp.zeros((cycle_dev, blocks * LON_SLOW), jnp.float32).at[:, target].set(returned[1])
    )
    field = inverse_field(full_real, full_imag, LON_SLOW, LON_FAST)
    cycles_all = cycle_dev * lat_count * ord_count
    return field * math.sqrt(cycles_all / (DEG * ORDERS))


def solution(mesh):
    return jax.shard_map(
        local,
        mesh=mesh,
        in_specs=(P(("lat", "ord"), None), P("lat", "ord", None), P(), P("ord")),
        out_specs=P(("lat", "ord"), None),
        check_vma=False,
    )
```

profile of v0, /device:TPU:1, one launch (start us, length us, event | category | flops | bytes accessed | tf_op | source)
XLA Modules:
  0.0 486.3 jit_solution(7475713609874748307)
XLA Ops:
  6.5 1.8 convert_multiply_fusion.1
  8.5 3.5 pad_maximum_fusion.1
  12.1 11.4 %reshape.129 = f32[48,180,240]{2,1,0:T(8,128)} reshape(f32[48,43200]{1,0:T(8,128)} %pad_maximum_fusion.1) | data formatting | bytes 16588800 | tf_op jit(solution)/shard_map/reshape | solution.py:33
  23.5 13.0 %convolution_bitcast_fusion = f32[48,180,240]{2,1,0:T(8,128)S(1)} fusion(f32[48,180,240]{2,1,0:T(8,128)} %reshape.129), kind=kOutput, calls=%fused_computation.48 | convolution fusion | flops 4479267840 | bytes 16588800 | tf_op jit(solution)/shard_map/raj,ak->rkj/dot_general | solution.py:35
  36.5 10.0 %negate_bitcast_fusion = f32[48,180,240]{2,1,0:T(8,128)S(1)} fusion(f32[48,180,240]{2,1,0:T(8,128)S(1)} %copy-done), kind=kOutput, calls=%fused_computation.26 | convolution fusion | flops 4481341440 | bytes 16588800 | tf_op jit(solution)/shard_map/raj,ak->rkj/dot_general | solution.py:36
  46.5 7.9 %pad_maximum_fusion = f32[48,180,480]{2,1,0:T(8,128)} fusion(f32[48,180,240]{2,1,0:T(8,128)S(1)} %negate_bitcast_fusion, f32[48,180,240]{2,1,0:T(8,128)S(1)} %convolution_bitcast_fusion), kind=kLoop, calls=%fused_computation.24 | loop fusion | flops 4147200 | bytes 33177600 | tf_op jit(solution)/shard_map/concatenate | solution.py:39
  54.4 26.4 %fusion.50 = (f32[180,240,29]{1,2,0:T(8,128)}, f32[180,240,29]{1,2,0:T(8,128)}, f32[180,240,29]{1,2,0:T(8,128)}) fusion(s32[240,29]{0,1:T(8,128)S(1)} %iota_multiply_fusion.1, s32[180,240]{1,0:T(8,128)S(1)} %iota_multiply_fusion), kind=kLoop, calls=%fused_computation.60 | loop fusion | flops 12528000 | bytes 15234240 | tf_op jit(solution)/shard_map/neg | solution.py:41
  80.8 38.7 %fusion.42 = f32[48,180,58]{2,0,1:T(8,128)S(1)} fusion(f32[48,180,480]{2,1,0:T(8,128)} %pad_maximum_fusion, f32[180,240,29]{1,2,0:T(8,128)} %get-tuple-element.15, f32[180,240,29]{1,2,0:T(8,128)} %get-tuple-element.14, f32[180,240,29]{1,2,0:T(8,128)} %get-tuple-element.13), kind=kOutput, calls=%fused_computation.57 | convolution fusion | flops 2901484800 | bytes 33626880 | tf_op jit(solution)/shard_map/rkj,kjq->rkq/dot_general | solution.py:43
  119.6 4.8 slice_bitcast_fusion.1
  124.4 4.4 copy.110
  128.8 1.7 reshape.173
  130.5 2.1 slice_multiply_fusion.1
  132.6 15.1 %gather_fusion = bf16[5120,48]{1,0:T(8,128)(2,1)S(1)} fusion(bf16[48,5120]{0,1:T(8,128)(2,1)S(1)} %slice_multiply_fusion.1, s32[5120]{0:T(1024)S(1)} %get-tuple-element.19), kind=kCustom, calls=%fused_computation | custom fusion | bytes 1003520 | tf_op jit(solution)/shard_map/gather | solution.py:95
  147.7 0.6 copy.85
  148.3 4.4 copy.111
  152.7 1.7 reshape.174
  154.4 2.1 slice_multiply_fusion
  156.5 15.1 %gather_fusion.1 = bf16[5120,48]{1,0:T(8,128)(2,1)S(1)} fusion(bf16[48,5120]{0,1:T(8,128)(2,1)S(1)} %slice_multiply_fusion, s32[5120]{0:T(1024)S(1)} %get-tuple-element.19), kind=kCustom, calls=%fused_computation.1 | custom fusion | bytes 1003520 | tf_op jit(solution)/shard_map/gather | solution.py:96
  172.4 8.2 %copy.90 = bf16[6,16,5120]{1,0,2:T(8,128)(2,1)} copy(bf16[6,16,5120]{2,1,0:T(8,128)(2,1)S(1)} %bitcast.72) | data formatting | bytes 1966080 | tf_op jit(solution)/shard_map/convert_element_type | solution.py:100
  180.6 11.5 %reshape.179 = bf16[8,2,30720]{2,1,0:T(2,128)(2,1)} reshape(bf16[5120,6,16]{2,1,0:T(8,128)(2,1)} %bitcast.69) | data formatting | bytes 1966080
  192.0 6.4 %all-to-all-start = ((bf16[8,2,30720]{2,1,0:T(2,128)(2,1)}), bf16[8,2,30720]{2,1,0:T(2,128)(2,1)S(1)}, u32[]{:S(2)}, u32[]{:S(2)}) async-start(bf16[8,2,30720]{2,1,0:T(2,128)(2,1)} %reshape.179), calls=%async_computation | async-start | bytes 1966080 | tf_op jit(solution)/shard_map/all_to_all | solution.py:103
  198.4 24.2 %all-to-all-done = bf16[8,2,30720]{2,1,0:T(2,128)(2,1)S(1)} async-done(((bf16[8,2,30720]{2,1,0:T(2,128)(2,1)}), bf16[8,2,30720]{2,1,0:T(2,128)(2,1)S(1)}, u32[]{:S(2)}, u32[]{:S(2)}) %all-to-all-start) | async-done | bytes 983072 | tf_op jit(solution)/shard_map/all_to_all | solution.py:103
  222.6 11.0 %reshape.180 = bf16[5120,6,16]{2,1,0:T(8,128)(2,1)} reshape(bf16[8,2,30720]{2,1,0:T(2,128)(2,1)S(1)} %all-to-all-done) | data formatting | bytes 1966080
  233.6 8.5 %copy.92 = bf16[6,8,16,640]{3,2,1,0:T(8,128)(2,1)S(1)} copy(bf16[6,8,16,640]{2,0,3,1:T(8,128)(2,1)} %bitcast.70) | data formatting | bytes 1966080 | tf_op jit(solution)/shard_map/all_to_all | solution.py:103
  242.0 1.4 copy.93
  243.4 26.1 %fusion.51 = f32[6,640,128]{2,0,1:T(8,128)S(1)} fusion(bf16[6,128,640]{1,0,2:T(8,128)(2,1)S(1)} %copy.93, bf16[128,640,128]{2,1,0:T(8,128)(2,1)} %param.5), kind=kOutput, calls=%fused_computation.61 | convolution fusion | flops 125829120 | bytes 23920640 | tf_op jit(solution)/shard_map/xrk,rkn->xkn/dot_general | solution.py:101
  269.8 1.0 multiply_reduce_fusion
  271.0 45.9 %all-reduce.2.cloned.1.call-done = f32[2,640,128]{2,1,0:T(8,128)} async-done(((f32[2,640,128]{2,1,0:T(8,128)}), f32[2,640,128]{2,1,0:T(8,128)}) %all-reduce.2.cloned.1.call-update) | async-done | bytes 655376 | tf_op jit(solution)/shard_map/psum | solution.py:119
  317.0 1.1 multiply_convert_fusion
  318.1 50.4 %fusion.61 = f32[2,128,640]{1,0,2:T(2,128)S(1)} fusion(bf16[128,640,128]{2,1,0:T(8,128)(2,1)} %param.5, bf16[2,640,128]{2,1,0:T(8,128)(2,1)S(1)} %multiply_convert_fusion), kind=kOutput, calls=%fused_computation.73 | convolution fusion | flops 41943040 | bytes 21954560 | tf_op jit(solution)/shard_map/rkn,ckn->crk/dot_general | solution.py:121
  368.5 1.4 copy.98
  369.9 5.3 %all-to-all-start.1 = ((f32[2,128,640]{2,0,1:T(2,128)}), f32[2,128,640]{2,0,1:T(2,128)S(1)}, u32[]{:S(2)}, u32[]{:S(2)}) async-start(f32[2,128,640]{2,0,1:T(2,128)} %copy.98), calls=%async_computation.1 | async-start | bytes 1310720 | tf_op jit(solution)/shard_map/all_to_all | solution.py:122
  375.2 26.6 %fusion.31 = (f32[180,29,240]{2,1,0:T(8,128)}, f32[180,29,240]{2,1,0:T(8,128)}, f32[180,29,240]{2,1,0:T(8,128)}) fusion(s32[29,240]{1,0:T(8,128)S(1)} %iota_multiply_fusion.2, s32[180,240]{1,0:T(8,128)S(1)} %iota_multiply_fusion), kind=kLoop, calls=%fused_computation.42 | loop fusion | flops 12528000 | bytes 15234240 | tf_op jit(solution)/shard_map/sin | solution.py:28
  401.9 2.2 copy.101
  404.2 14.0 %scatter_custom_fusion = f32[16,5220]{0,1:T(8,128)S(1)} fusion(s32[5120]{0:T(1024)S(1)} %get-tuple-element.20, f32[5120,16]{1,0:T(8,128)} %copy.101, f32[]{:T(128)} %constant.52.clone.1), kind=kCustom, calls=%fused_computation.69 | custom fusion | bytes 334592 | tf_op jit(solution)/shard_map/scatter | solution.py:126
  418.2 0.7 copy.102
  419.0 0.7 reshape.133
  419.6 2.0 copy.103
  421.7 2.2 copy.105
  423.9 14.0 %scatter_custom_fusion.1 = f32[16,5220]{0,1:T(8,128)S(1)} fusion(s32[5120]{0:T(1024)S(1)} %get-tuple-element.20, f32[5120,16]{1,0:T(8,128)} %copy.105, f32[]{:T(128)} %constant.52.clone.1), kind=kCustom, calls=%fused_computation.67 | custom fusion | bytes 334592 | tf_op jit(solution)/shard_map/scatter | solution.py:129
  438.0 0.7 copy.106
  438.7 0.7 reshape.134
  439.4 2.0 copy.107
  441.4 24.1 %fusion.39 = f32[16,180,480]{2,0,1:T(8,128)S(1)} fusion(f32[180,29,240]{2,1,0:T(8,128)} %get-tuple-element.18, f32[180,29,240]{2,1,0:T(8,128)} %get-tuple-element.17, f32[180,29,240]{2,1,0:T(8,128)} %get-tuple-element.16, f32[16,180,29]{2,0,1:T(8,128)} %bitcast.80, f32[16,180,29]{2,0,1:T(8,128)} %bitcast.79), kind=kOutput, calls=%fused_computation.56 | convolution fusion | flops 977351040 | bytes 21231360 | tf_op jit(solution)/shard_map/rkq,kqj->rkj/dot_general | solution.py:70
  465.5 1.1 fusion.108
  466.6 4.9 %fusion.35 = f32[180,16,240]{2,0,1:T(8,128)S(1)} fusion(f32[16,180,240]{2,0,1:T(8,128)S(1)} %get-tuple-element.6), kind=kOutput, calls=%fused_computation.49 | convolution fusion | flops 1493283584 | bytes 5529600 | tf_op jit(solution)/shard_map/rkj,ka->raj/dot_general | solution.py:73
  471.5 5.1 %multiply_bitcast_fusion = f32[16,180,240]{2,1,0:T(8,128)S(1)} fusion(f32[180,16,240]{2,0,1:T(8,128)S(1)} %fusion.35, f32[16,180,240]{2,0,1:T(8,128)S(1)} %get-tuple-element.5), kind=kOutput, calls=%fused_computation.53 | convolution fusion | flops 1494665984 | bytes 8294400 | tf_op jit(solution)/shard_map/rkj,ka->raj/dot_general | solution.py:72
  476.6 2.5 mul.334
  (30 shorter events, 1.7 us)
Async XLA Ops:
  6.5 1.8 copy-start.1
  23.5 13.0 %copy-start = (f32[48,180,240]{2,1,0:T(8,128)S(1)}, f32[48,180,240]{2,1,0:T(8,128)}, u32[]{:S(2)}) copy-start(f32[48,180,240]{2,1,0:T(8,128)} %reshape.129) | copy-start | bytes 24883204
  128.8 3.8 copy-start.2
  192.0 30.6 %all-to-all-start = ((bf16[8,2,30720]{2,1,0:T(2,128)(2,1)}), bf16[8,2,30720]{2,1,0:T(2,128)(2,1)S(1)}, u32[]{:S(2)}, u32[]{:S(2)}) async-start(bf16[8,2,30720]{2,1,0:T(2,128)(2,1)} %reshape.179), calls=%async_computation | async-start | bytes 1966080 | tf_op jit(solution)/shard_map/all_to_all | solution.py:103
  198.4 118.6 %all-reduce.2.cloned.1.call-start = ((), (), s32[]{:S(2)}) async-start(), calls=%async_computation.2 | async-start | bytes 1310720 | tf_op jit(solution)/shard_map/psum | solution.py:119
  269.4 1.4 copy-start.3
  369.9 32.0 %all-to-all-start.1 = ((f32[2,128,640]{2,0,1:T(2,128)}), f32[2,128,640]{2,0,1:T(2,128)S(1)}, u32[]{:S(2)}, u32[]{:S(2)}) async-start(f32[2,128,640]{2,0,1:T(2,128)} %copy.98), calls=%async_computation.1 | async-start | bytes 1310720 | tf_op jit(solution)/shard_map/all_to_all | solution.py:122
Sparse Core Ops, SparseCore 0:
  271.0 45.9 all-reduce.1
where the time goes:
time: 493 us; the launch traced here: 486 us
  matrix products  172 us (35%)
  local copies, waits for them, and re-layouts  145 us (29%)
  other arithmetic  73.1 us (15%)
  waiting for transfers between devices  70.1 us (14%)
  between operations  14 us (3%)
  starting transfers between devices  11.7 us (2%)
    dot_general x1, matrix products, local(): jnp.einsum('rkn,ckn->crk', panels, coeffs, preferred_element_type=jnp.flo...  50.4 us
    psum x1, waiting for transfers between devices, local(): total = lax.psum(terms, 'lat')  45.9 us
    dot_general x1, matrix products, forward_spectra(): jnp.einsum('rkj,kjq->rkq', joined, table, precision=lax.Precision.HIGHEST)  38.7 us
    scatter x4, local copies, waits for them, and re-layouts, local(): jnp.zeros((cycle_dev, blocks * LON_SLOW), jnp.float32).at[:, target]  29.5 us
    sin x1, other arithmetic, twiddle_tables(): return (jnp.cos(angle), jnp.sin(angle))  26.6 us
    neg x1, other arithmetic, forward_spectra(): -twist_sin  26.4 us
    dot_general x1, matrix products, local(): jnp.einsum('xrk,rkn->xkn', lax.all_to_all(picked, 'ord', split_axis=2, co...  26.1 us
    all_to_all x1, waiting for transfers between devices, local(): lax.all_to_all(picked, 'ord', split_axis=2, concat_axis=1, tiled=True)  24.2 us
  transfers between devices with their start and end apart: 3, of which 2 were waited for; matrix products, arithmetic and copies ran while one was open for 6% of the time, Pallas kernels for 0%

commit v1 on v0

--- a/solution.py
+++ b/solution.py
@@ -9,6 +9,12 @@
 ORDERS = 5120
 DEG = 128
 NMAX = 21600
+
+
+def swap_blocks(x, mesh_axis, split, join):
+    pieces = jnp.split(x, lax.axis_size(mesh_axis), axis=split)
+    incoming = lax.all_to_all(jnp.stack(pieces), mesh_axis, 0, 0)
+    return jnp.concatenate(incoming, axis=join)
 
 
 def slow_tables(slow):
@@ -99,10 +105,7 @@
     )
     picked = picked.reshape(6, cycle_dev, ORDERS).astype(jnp.bfloat16)
     sums = jnp.einsum(
-        "xrk,rkn->xkn",
-        lax.all_to_all(picked, "ord", split_axis=2, concat_axis=1, tiled=True),
-        panels,
-        preferred_element_type=jnp.float32,
+        "xrk,rkn->xkn", swap_blocks(picked, "ord", 2, 1), panels, preferred_element_type=jnp.float32
     )
     stride = (NMAX - ORDERS) // DEG
     degree_int = ORDERS + jnp.arange(DEG, dtype=jnp.int32) * stride

time: 493 us -> 459 us (0.931)
  local copies, waits for them, and re-layouts: 145 us -> 112 us
    unnamed x12 -> x17, local copies, waits for them, and re-layouts: 22.5 us -> 4.69 us
    all_to_all x2 -> x0, local copies, waits for them, and re-layouts: 9.82 us -> none  [local(): lax.all_to_all(picked, 'ord', split_axis=2, concat_axis=1, tiled=True)]
    convert_element_type x1 -> x0, local copies, waits for them, and re-layouts: 8.16 us -> none  [local(): picked = picked.reshape(6, cycle_dev, ORDERS).astype(jnp.bfloat16)]
where the time goes in v1:
time: 459 us; the launch traced here: 453 us
  matrix products  172 us (37%)
  local copies, waits for them, and re-layouts  112 us (24%)
  other arithmetic  73.1 us (16%)
  waiting for transfers between devices  70.1 us (15%)
  between operations  14 us (3%)
  starting transfers between devices  11.7 us (3%)
    dot_general x1, matrix products, local(): jnp.einsum('rkn,ckn->crk', panels, coeffs, preferred_element_type=jnp.flo...  50.4 us
    psum x1, waiting for transfers between devices, local(): total = lax.psum(terms, 'lat')  45.9 us
    dot_general x1, matrix products, forward_spectra(): jnp.einsum('rkj,kjq->rkq', joined, table, precision=lax.Precision.HIGHEST)  38.5 us
    scatter x4, local copies, waits for them, and re-layouts, local(): jnp.zeros((cycle_dev, blocks * LON_SLOW), jnp.float32).at[:, target]  29.5 us
    sin x1, other arithmetic, twiddle_tables(): return (jnp.cos(angle), jnp.sin(angle))  26.6 us
    neg x1, other arithmetic, forward_spectra(): -twist_sin  26.4 us
    dot_general x1, matrix products, local(): jnp.einsum('xrk,rkn->xkn', swap_blocks(picked, 'ord', 2, 1), panels, pref...  26.1 us
    all_to_all x1, waiting for transfers between devices, swap_blocks(): incoming = lax.all_to_all(jnp.stack(pieces), mesh_axis, 0, 0)  24.2 us
  transfers between devices with their start and end apart: 3, of which 2 were waited for; matrix products, arithmetic and copies ran while one was open for 6% of the time, Pallas kernels for 0%

profile of v1, /device:TPU:1, one launch (start us, length us, event | category | flops | bytes accessed | tf_op | source)
XLA Modules:
  0.0 452.8 jit_solution(8767919722951703207)
XLA Ops:
  6.5 1.8 convert_multiply_fusion.1
  8.5 3.5 pad_maximum_fusion.1
  12.1 11.4 %reshape.135 = f32[48,180,240]{2,1,0:T(8,128)} reshape(f32[48,43200]{1,0:T(8,128)} %pad_maximum_fusion.1) | data formatting | bytes 16588800 | tf_op jit(solution)/shard_map/reshape | solution.py:39
  23.5 13.0 %convolution_bitcast_fusion = f32[48,180,240]{2,1,0:T(8,128)S(1)} fusion(f32[48,180,240]{2,1,0:T(8,128)} %reshape.135), kind=kOutput, calls=%fused_computation.48 | convolution fusion | flops 4479267840 | bytes 16588800 | tf_op jit(solution)/shard_map/raj,ak->rkj/dot_general | solution.py:41
  36.5 10.0 %negate_bitcast_fusion = f32[48,180,240]{2,1,0:T(8,128)S(1)} fusion(f32[48,180,240]{2,1,0:T(8,128)S(1)} %copy-done), kind=kOutput, calls=%fused_computation.26 | convolution fusion | flops 4481341440 | bytes 16588800 | tf_op jit(solution)/shard_map/raj,ak->rkj/dot_general | solution.py:42
  46.5 7.9 %pad_maximum_fusion = f32[48,180,480]{2,1,0:T(8,128)} fusion(f32[48,180,240]{2,1,0:T(8,128)S(1)} %negate_bitcast_fusion, f32[48,180,240]{2,1,0:T(8,128)S(1)} %convolution_bitcast_fusion), kind=kLoop, calls=%fused_computation.24 | loop fusion | flops 4147200 | bytes 33177600 | tf_op jit(solution)/shard_map/concatenate | solution.py:45
  54.4 26.4 %fusion.50 = (f32[180,240,29]{1,2,0:T(8,128)}, f32[180,240,29]{1,2,0:T(8,128)}, f32[180,240,29]{1,2,0:T(8,128)}) fusion(s32[240,29]{0,1:T(8,128)S(1)} %iota_multiply_fusion.1, s32[180,240]{1,0:T(8,128)S(1)} %iota_multiply_fusion), kind=kLoop, calls=%fused_computation.60 | loop fusion | flops 12528000 | bytes 15234240 | tf_op jit(solution)/shard_map/neg | solution.py:47
  80.8 38.5 %fusion.42 = f32[48,180,58]{2,0,1:T(8,128)S(1)} fusion(f32[48,180,480]{2,1,0:T(8,128)} %pad_maximum_fusion, f32[180,240,29]{1,2,0:T(8,128)} %get-tuple-element.15, f32[180,240,29]{1,2,0:T(8,128)} %get-tuple-element.14, f32[180,240,29]{1,2,0:T(8,128)} %get-tuple-element.13), kind=kOutput, calls=%fused_computation.57 | convolution fusion | flops 2901484800 | bytes 33626880 | tf_op jit(solution)/shard_map/rkj,kjq->rkq/dot_general | solution.py:49
  119.4 4.8 %slice_bitcast_fusion.1 = (f32[48,29,180]{1,0,2:T(8,128)}, f32[48,29,180]{1,0,2:T(8,128)}) fusion(f32[48,180,58]{2,0,1:T(8,128)S(1)} %fusion.42), kind=kLoop, calls=%fused_computation.47 | loop fusion | bytes 4008960 | tf_op jit(solution)/shard_map/transpose | solution.py:52
  124.2 4.4 copy.114
  128.6 1.7 reshape.181
  130.3 2.1 slice_multiply_fusion.1
  132.4 15.1 %gather_fusion = bf16[5120,48]{1,0:T(8,128)(2,1)S(1)} fusion(bf16[48,5120]{0,1:T(8,128)(2,1)S(1)} %slice_multiply_fusion.1, s32[5120]{0:T(1024)S(1)} %get-tuple-element.19), kind=kCustom, calls=%fused_computation | custom fusion | bytes 1003520 | tf_op jit(solution)/shard_map/gather | solution.py:101
  148.1 4.9 %copy.115 = f32[48,29,180]{0,2,1:T(8,128)S(1)} copy(f32[48,29,180]{1,0,2:T(8,128)} %get-tuple-element.8) | data formatting | bytes 2004480 | tf_op jit(solution)/shard_map/reshape | solution.py:55
  153.0 1.7 reshape.182
  154.7 2.1 slice_multiply_fusion
  156.8 15.1 %gather_fusion.1 = bf16[5120,48]{1,0:T(8,128)(2,1)S(1)} fusion(bf16[48,5120]{0,1:T(8,128)(2,1)S(1)} %slice_multiply_fusion, s32[5120]{0:T(1024)S(1)} %get-tuple-element.19), kind=kCustom, calls=%fused_computation.1 | custom fusion | bytes 1003520 | tf_op jit(solution)/shard_map/gather | solution.py:102
  172.7 0.7 fusion.87
  173.3 0.7 fusion.86
  174.0 0.7 fusion.85
  174.7 0.7 fusion.84
  175.3 0.7 fusion.83
  178.0 6.4 %all-to-all-start = ((bf16[8,6,16,640]{3,2,1,0:T(8,128)(2,1)}), bf16[8,6,16,640]{3,2,1,0:T(8,128)(2,1)S(1)}, u32[]{:S(2)}, u32[]{:S(2)}) async-start(bf16[8,6,16,640]{3,2,1,0:T(8,128)(2,1)} %fusion.80), calls=%async_computation | async-start | bytes 1966080 | tf_op jit(solution)/shard_map/all_to_all | solution.py:16
  184.4 24.2 %all-to-all-done = bf16[8,6,16,640]{3,2,1,0:T(8,128)(2,1)S(1)} async-done(((bf16[8,6,16,640]{3,2,1,0:T(8,128)(2,1)}), bf16[8,6,16,640]{3,2,1,0:T(8,128)(2,1)S(1)}, u32[]{:S(2)}, u32[]{:S(2)}) %all-to-all-start) | async-done | bytes 983072 | tf_op jit(solution)/shard_map/all_to_all | solution.py:16
  208.6 1.4 copy.97
  210.0 26.1 %fusion.51 = f32[6,640,128]{2,0,1:T(8,128)S(1)} fusion(bf16[6,128,640]{1,0,2:T(8,128)(2,1)S(1)} %copy.97, bf16[128,640,128]{2,1,0:T(8,128)(2,1)} %param.5), kind=kOutput, calls=%fused_computation.61 | convolution fusion | flops 125829120 | bytes 23920640 | tf_op jit(solution)/shard_map/xrk,rkn->xkn/dot_general | solution.py:107
  236.4 1.0 multiply_reduce_fusion
  237.6 45.9 %all-reduce.2.cloned.1.call-done = f32[2,640,128]{2,1,0:T(8,128)} async-done(((f32[2,640,128]{2,1,0:T(8,128)}), f32[2,640,128]{2,1,0:T(8,128)}) %all-reduce.2.cloned.1.call-update) | async-done | bytes 655376 | tf_op jit(solution)/shard_map/psum | solution.py:122
  283.5 1.1 multiply_convert_fusion
  284.7 50.4 %fusion.61 = f32[2,128,640]{1,0,2:T(2,128)S(1)} fusion(bf16[128,640,128]{2,1,0:T(8,128)(2,1)} %param.5, bf16[2,640,128]{2,1,0:T(8,128)(2,1)S(1)} %multiply_convert_fusion), kind=kOutput, calls=%fused_computation.73 | convolution fusion | flops 41943040 | bytes 21954560 | tf_op jit(solution)/shard_map/rkn,ckn->crk/dot_general | solution.py:124
  335.1 1.4 copy.102
  336.5 5.3 %all-to-all-start.1 = ((f32[2,128,640]{2,0,1:T(2,128)}), f32[2,128,640]{2,0,1:T(2,128)S(1)}, u32[]{:S(2)}, u32[]{:S(2)}) async-start(f32[2,128,640]{2,0,1:T(2,128)} %copy.102), calls=%async_computation.1 | async-start | bytes 1310720 | tf_op jit(solution)/shard_map/all_to_all | solution.py:125
  341.8 26.6 %fusion.31 = (f32[180,29,240]{2,1,0:T(8,128)}, f32[180,29,240]{2,1,0:T(8,128)}, f32[180,29,240]{2,1,0:T(8,128)}) fusion(s32[29,240]{1,0:T(8,128)S(1)} %iota_multiply_fusion.2, s32[180,240]{1,0:T(8,128)S(1)} %iota_multiply_fusion), kind=kLoop, calls=%fused_computation.42 | loop fusion | flops 12528000 | bytes 15234240 | tf_op jit(solution)/shard_map/sin | solution.py:34
  368.5 2.2 copy.105
  370.8 14.0 %scatter_custom_fusion = f32[16,5220]{0,1:T(8,128)S(1)} fusion(s32[5120]{0:T(1024)S(1)} %get-tuple-element.20, f32[5120,16]{1,0:T(8,128)} %copy.105, f32[]{:T(128)} %constant.52.clone.1), kind=kCustom, calls=%fused_computation.69 | custom fusion | bytes 334592 | tf_op jit(solution)/shard_map/scatter | solution.py:129
  384.8 0.7 copy.106
  385.6 0.7 reshape.141
  386.2 2.0 copy.107
  388.3 2.2 copy.109
  390.5 14.0 %scatter_custom_fusion.1 = f32[16,5220]{0,1:T(8,128)S(1)} fusion(s32[5120]{0:T(1024)S(1)} %get-tuple-element.20, f32[5120,16]{1,0:T(8,128)} %copy.109, f32[]{:T(128)} %constant.52.clone.1), kind=kCustom, calls=%fused_computation.67 | custom fusion | bytes 334592 | tf_op jit(solution)/shard_map/scatter | solution.py:132
  404.6 0.7 copy.110
  405.3 0.7 reshape.142
  406.0 2.0 copy.111
  408.0 24.0 %fusion.39 = f32[16,180,480]{2,0,1:T(8,128)S(1)} fusion(f32[180,29,240]{2,1,0:T(8,128)} %get-tuple-element.18, f32[180,29,240]{2,1,0:T(8,128)} %get-tuple-element.17, f32[180,29,240]{2,1,0:T(8,128)} %get-tuple-element.16, f32[16,180,29]{2,0,1:T(8,128)} %bitcast.113, f32[16,180,29]{2,0,1:T(8,128)} %bitcast.112), kind=kOutput, calls=%fused_computation.56 | convolution fusion | flops 977351040 | bytes 21231360 | tf_op jit(solution)/shard_map/rkq,kqj->rkj/dot_general | solution.py:76
  432.0 1.1 fusion.116
  433.1 4.9 %fusion.35 = f32[180,16,240]{2,0,1:T(8,128)S(1)} fusion(f32[16,180,240]{2,0,1:T(8,128)S(1)} %get-tuple-element.6), kind=kOutput, calls=%fused_computation.49 | convolution fusion | flops 1493283584 | bytes 5529600 | tf_op jit(solution)/shard_map/rkj,ka->raj/dot_general | solution.py:79
  438.0 5.1 %multiply_bitcast_fusion = f32[16,180,240]{2,1,0:T(8,128)S(1)} fusion(f32[180,16,240]{2,0,1:T(8,128)S(1)} %fusion.35, f32[16,180,240]{2,0,1:T(8,128)S(1)} %get-tuple-element.5), kind=kOutput, calls=%fused_computation.53 | convolution fusion | flops 1494665984 | bytes 8294400 | tf_op jit(solution)/shard_map/rkj,ka->raj/dot_general | solution.py:78
  443.2 2.5 mul.334
  (35 shorter events, 4.3 us)
Async XLA Ops:
  6.5 1.8 copy-start.1
  23.5 13.0 %copy-start = (f32[48,180,240]{2,1,0:T(8,128)S(1)}, f32[48,180,240]{2,1,0:T(8,128)}, u32[]{:S(2)}) copy-start(f32[48,180,240]{2,1,0:T(8,128)} %reshape.135) | copy-start | bytes 24883204
  128.6 3.8 copy-start.2
  178.0 30.6 %all-to-all-start = ((bf16[8,6,16,640]{3,2,1,0:T(8,128)(2,1)}), bf16[8,6,16,640]{3,2,1,0:T(8,128)(2,1)S(1)}, u32[]{:S(2)}, u32[]{:S(2)}) async-start(bf16[8,6,16,640]{3,2,1,0:T(8,128)(2,1)} %fusion.80), calls=%async_computation | async-start | bytes 1966080 | tf_op jit(solution)/shard_map/all_to_all | solution.py:16
  184.3 99.2 %all-reduce.2.cloned.1.call-start = ((), (), s32[]{:S(2)}) async-start(), calls=%async_computation.2 | async-start | bytes 1310720 | tf_op jit(solution)/shard_map/psum | solution.py:122
  236.0 1.4 copy-start.3
  336.5 32.0 %all-to-all-start.1 = ((f32[2,128,640]{2,0,1:T(2,128)}), f32[2,128,640]{2,0,1:T(2,128)S(1)}, u32[]{:S(2)}, u32[]{:S(2)}) async-start(f32[2,128,640]{2,0,1:T(2,128)} %copy.102), calls=%async_computation.1 | async-start | bytes 1310720 | tf_op jit(solution)/shard_map/all_to_all | solution.py:125
Sparse Core Ops, SparseCore 0:
  237.6 45.9 all-reduce.1
